TPU v7x, 32 devices: a whole 2x2x4 slice. The times are simulated.
32 devices in a mesh: exp: 16 (over z, y, core), ctx: 2 (over x).
Axes of the slice: x: 2, y: 2, z: 4, core: 2. Of those that a mesh axis runs over, the one named last changes fastest.
Arguments:
- inputs: bfloat16 [4096, 1024], P(('exp', 'ctx')), may hold values from -30 to 30
- selected: int32 [32, 32], P(None, 'ctx'), may hold values from 0 to 4095, as said below
- selection_gate: float32 [32, 32], P('exp', 'ctx'), may hold values from 0.1 to 1
- gate_weight: bfloat16 [32, 1024, 2048], P('exp', None, 'ctx'), may hold values from -0.1875 to 0.1875
- up_weight: bfloat16 [32, 1024, 2048], P('exp', None, 'ctx'), may hold values from -0.1875 to 0.1875
- down_weight: bfloat16 [32, 2048, 1024], P('exp', 'ctx'), may hold values from -0.125 to 0.125
- norm_gain: float32 [1024], replicated, may hold values from 0.5 to 1.5
- query_weight: bfloat16 [1024, 1024], P('exp'), may hold values from -1 to 1
- key_weight: bfloat16 [1024, 1024], P('exp'), may hold values from -1 to 1
- value_weight: bfloat16 [1024, 1024], P('exp'), may hold values from -0.1875 to 0.1875
- train_count: int32 [16], P('exp'), may hold values from 64 to 255
Outputs:
- layer_out: bfloat16 [4096, 1024], P(('exp', 'ctx'))
- context: bfloat16 [4096, 1024], P(('exp', 'ctx'))
Inputs may be any that keep to these rules, and one draw needn't show every extreme that they name: `selected`: each expert's 32 entries are distinct rows. Entries c * 16 to (c + 1) * 16 - 1 of every expert name rows at positions c * 128 to (c + 1) * 128 - 1 of their tables. At most 2 entries of one expert name rows of one block of 128 rows, and in each group of 16 entries of each expert some block gives exactly 2.
All inputs are finite; a program needn't handle non-finite values.
Results may differ from a plain program's by a relative error of at most 0.017.
Values may be sent and summed in bfloat16 or wider, within the bound.
A program may use at most 64 MiB of HBM per device.

v0:
```python
import jax
import jax.numpy as jnp
from jax import lax
from jax.sharding import PartitionSpec as P

HEAD_DIM = 64


EPSILON = 1e-06
MASKED = -1e30


def block_rank(block_ids):
    slot_count = block_ids.shape[1]
    earlier = jnp.arange(slot_count)[:, None] > jnp.arange(slot_count)[None, :]
    same_block = block_ids[:, :, None] == block_ids[:, None, :]
    return jnp.sum(jnp.where(same_block & earlier[None], 1, 0), axis=2).astype(jnp.int32)


def local(
    inputs,
    selected,
    selection_gate,
    gate_weight,
    up_weight,
    down_weight,
    norm_gain,
    query_weight,
    key_weight,
    value_weight,
    train_count,
):
    exp_count = lax.axis_size("exp")
    ctx_count = lax.axis_size("ctx")
    exp_index = lax.axis_index("exp")
    ctx_index = lax.axis_index("ctx")
    row_count, model_width = inputs.shape
    expert_local = gate_weight.shape[0]
    group_take = selected.shape[1]
    most_rows = max(2, (2 * group_take + exp_count - 1) // exp_count)
    block_ids = selected // row_count
    slot_rank = block_rank(block_ids)
    own_block = exp_index * ctx_count + ctx_index
    is_mine = block_ids == own_block
    local_row = selected - own_block * row_count
    rank_slots = jnp.arange(most_rows, dtype=jnp.int32)
    slot_hit = is_mine[:, None, :] & (slot_rank[:, None, :] == rank_slots[None, :, None])
    pick_row = jnp.sum(jnp.where(slot_hit, local_row[:, None, :], 0), axis=2)
    filled = jnp.any(slot_hit, axis=2).reshape(-1)
    picked = jnp.take(inputs, pick_row.reshape(-1), axis=0)
    outgoing = jnp.where(filled[:, None], picked, jnp.zeros_like(picked)).reshape(
        exp_count, -1, model_width
    )
    incoming = lax.all_to_all(outgoing, "exp", split_axis=0, concat_axis=0, tiled=True)
    my_blocks = lax.dynamic_slice_in_dim(block_ids, exp_index * expert_local, expert_local, 0)
    my_rank = lax.dynamic_slice_in_dim(slot_rank, exp_index * expert_local, expert_local, 0)
    my_source = my_blocks // ctx_count
    expert_slot = jnp.arange(expert_local, dtype=jnp.int32)[:, None]
    flat_index = (my_source * expert_local + expert_slot) * most_rows + my_rank
    compact = jnp.take(incoming.reshape(-1, model_width), flat_index.T.reshape(-1), axis=0)
    compact = compact.reshape(group_take, expert_local, model_width)
    block_rows = lax.all_gather(compact, "ctx", axis=0, tiled=True)
    gate_part = jnp.einsum(
        "nxd,xdf->nxf", block_rows, gate_weight, preferred_element_type=jnp.float32
    )
    up_part = jnp.einsum("nxd,xdf->nxf", block_rows, up_weight, preferred_element_type=jnp.float32)
    hidden = (jax.nn.silu(gate_part) * up_part).astype(jnp.bfloat16)
    summed = lax.psum_scatter(
        jnp.einsum("nxf,xfd->nxd", hidden, down_weight, preferred_element_type=jnp.float32).astype(
            jnp.bfloat16
        ),
        "ctx",
        scatter_dimension=0,
        tiled=True,
    ).astype(jnp.float32)
    weighted = (summed * selection_gate.T[:, :, None]).astype(jnp.bfloat16)
    source_ids = jnp.arange(exp_count, dtype=jnp.int32)
    expert_ids = jnp.arange(expert_local, dtype=jnp.int32)[None, :, None, None]
    slot_index = jnp.arange(group_take, dtype=jnp.int32)[None, None, None, :]
    reply_hit = (my_source[None, :, None, :] == source_ids[:, None, None, None]) & (
        my_rank[None, :, None, :] == rank_slots[None, None, :, None]
    )
    reply_pick = jnp.sum(jnp.where(reply_hit, slot_index * expert_local + expert_ids, 0), axis=3)
    reply_filled = jnp.any(reply_hit, axis=3).reshape(-1)
    reply_rows = jnp.take(weighted.reshape(-1, model_width), reply_pick.reshape(-1), axis=0)
    reply_rows = jnp.where(reply_filled[:, None], reply_rows, jnp.zeros_like(reply_rows)).reshape(
        exp_count, -1, model_width
    )
    returned = lax.all_to_all(reply_rows, "exp", split_axis=0, concat_axis=0, tiled=True)
    owner_hit = (
        pick_row.reshape(-1)[None, :] == jnp.arange(row_count, dtype=jnp.int32)[:, None]
    ) & filled[None, :]
    moe_sum = jnp.dot(
        owner_hit.astype(jnp.bfloat16),
        returned.reshape(-1, model_width),
        preferred_element_type=jnp.float32,
    )
    layer_out = (inputs.astype(jnp.float32) + moe_sum).astype(jnp.bfloat16)
    widened = layer_out.astype(jnp.float32)
    scale_row = lax.rsqrt(jnp.mean(widened * widened, axis=1, keepdims=True) + EPSILON)
    normed = (widened * scale_row * norm_gain).astype(jnp.bfloat16)
    score_scale = HEAD_DIM ** (-0.5)
    train_rows = train_count[0]
    head_cols = model_width // ctx_count
    col_start = ctx_index * head_cols
    query_cols = lax.dynamic_slice_in_dim(query_weight, col_start, head_cols, 1)
    key_cols = lax.dynamic_slice_in_dim(key_weight, col_start, head_cols, 1)
    value_cols = lax.dynamic_slice_in_dim(value_weight, col_start, head_cols, 1)
    gathered = (
        lax.all_gather(query_cols, "exp", axis=0, tiled=True),
        lax.all_gather(key_cols, "exp", axis=0, tiled=True),
        lax.all_gather(value_cols, "exp", axis=0, tiled=True),
    )
    joined = jnp.concatenate(gathered, axis=1)
    table_proj = jnp.dot(
        lax.all_gather(normed, "ctx", axis=0, tiled=True),
        joined,
        preferred_element_type=jnp.float32,
    ).astype(jnp.bfloat16)
    table_count = table_proj.shape[0]
    local_heads = head_cols // HEAD_DIM
    query_all = table_proj[:, :head_cols].reshape(table_count, local_heads, HEAD_DIM)
    key_all = table_proj[:, head_cols : 2 * head_cols].reshape(table_count, local_heads, HEAD_DIM)
    value_all = table_proj[:, 2 * head_cols :].reshape(table_count, local_heads, HEAD_DIM)
    block_size = min(table_count, 512)
    allowed = jnp.arange(table_count, dtype=jnp.int32) < train_rows

    def attend_block(query_block):
        scores = (
            jnp.einsum("qhd,khd->hqk", query_block, key_all, preferred_element_type=jnp.float32)
            * score_scale
        )
        scores = jnp.where(allowed, scores, MASKED)
        top_score = jnp.max(scores, axis=2, keepdims=True)
        weights = jnp.where(allowed, jnp.exp(scores - top_score), 0.0)
        denominator = jnp.sum(weights, axis=2)
        blended = jnp.einsum(
            "hqk,khd->qhd",
            weights.astype(jnp.bfloat16),
            value_all,
            preferred_element_type=jnp.float32,
        )
        return (blended / denominator.T[:, :, None]).astype(jnp.bfloat16)

    head_context = lax.map(
        attend_block,
        query_all.reshape(table_count // block_size, block_size, local_heads, HEAD_DIM),
    )
    context = lax.all_to_all(
        head_context.reshape(table_count, head_cols), "ctx", split_axis=0, concat_axis=1, tiled=True
    )
    return (layer_out, context)


def solution(mesh):
    placed = (
        P(("exp", "ctx"), None),
        P(None, "ctx"),
        P("exp", "ctx"),
        P("exp", None, "ctx"),
        P("exp", None, "ctx"),
        P("exp", "ctx", None),
        P(),
        P("exp", None),
        P("exp", None),
        P("exp", None),
        P("exp"),
    )
    return jax.shard_map(
        local,
        mesh=mesh,
        in_specs=placed,
        out_specs=(P(("exp", "ctx"), None), P(("exp", "ctx"), None)),
        check_vma=False,
    )
```

profile of v0, /device:TPU:0, one launch (start us, length us, event | category | flops | bytes accessed | tf_op | source)
XLA Modules:
  0.0 182.7 jit_solution(5891580414236807411)
XLA Ops:
  8.0 0.7 broadcast_compare_fusion
  8.8 0.7 broadcast_subtract_fusion
  10.6 1.8 gather_fusion
  12.6 0.8 select_select_fusion.1
  13.4 7.4 %all-to-all-start = ((bf16[16,4,1024]{2,1,0:T(4,128)(2,1)}), bf16[16,4,1024]{2,1,0:T(4,128)(2,1)S(1)}, u32[]{:S(2)}, u32[]{:S(2)}) async-start(bf16[16,4,1024]{2,1,0:T(4,128)(2,1)} %select_select_fusion.1), calls=%async_computation | async-start | bytes 262144 | tf_op jit(solution)/shard_map/all_to_all | solution.py:54
  21.1 7.7 %all-to-all-done = bf16[16,4,1024]{2,1,0:T(4,128)(2,1)S(1)} async-done(((bf16[16,4,1024]{2,1,0:T(4,128)(2,1)}), bf16[16,4,1024]{2,1,0:T(4,128)(2,1)S(1)}, u32[]{:S(2)}, u32[]{:S(2)}) %all-to-all-start) | async-done | bytes 131104 | tf_op jit(solution)/shard_map/all_to_all | solution.py:54
  29.5 4.9 %all_gather.15 = bf16[32,2,1024]{2,0,1:T(8,128)(2,1)S(1)} all-gather(bf16[16,2,1024]{2,0,1:T(8,128)(2,1)S(1)} %copy_select_fusion), channel_id=1, replica_groups=mesh['exp'=16,'ctx'=2] {'ctx'}, dimensions={0}, use_global_device_ids=true | all-gather | bytes 196608 | tf_op jit(solution)/shard_map/all_gather | solution.py:62
  34.5 3.0 %convolution_bitcast_fusion.2 = f32[32,2,1024]{2,0,1:T(8,128)S(1)} fusion(bf16[32,2,1024]{2,0,1:T(8,128)(2,1)S(1)} %all_gather.15, bf16[2,1024,1024]{2,1,0:T(8,128)(2,1)} %param.14), kind=kOutput, calls=%fused_computation.21 | convolution fusion | flops 134217728 | bytes 4587520 | tf_op jit(solution)/shard_map/nxd,xdf->nxf/dot_general | solution.py:63
  37.5 5.7 %fusion.16 = bf16[32,2,1024]{2,0,1:T(8,128)(2,1)} fusion(bf16[2,1024,1024]{2,1,0:T(8,128)(2,1)} %param.16, bf16[32,2,1024]{2,0,1:T(8,128)(2,1)S(1)} %all_gather.15, bf16[2,1024,1024]{2,1,0:T(8,128)(2,1)} %param.15, f32[32,2,1024]{2,0,1:T(8,128)S(1)} %convolution_bitcast_fusion.2), kind=kOutput, calls=%fused_computation.24 | convolution fusion | flops 268894208 | bytes 8912896 | tf_op jit(solution)/shard_map/nxf,xfd->nxd/dot_general | solution.py:69
  46.0 5.5 %reduce-scatter.2.cloned.1.call-done = bf16[16,2,1024]{2,0,1:T(8,128)(2,1)} async-done(((bf16[32,2,1024]{2,0,1:T(8,128)(2,1)}), bf16[16,2,1024]{2,0,1:T(8,128)(2,1)}) %reduce-scatter.2.cloned.1.call-update) | async-done | bytes 65552 | tf_op jit(solution)/shard_map/reduce_scatter | solution.py:68
  51.5 0.9 multiply_convert_fusion
  52.6 0.7 gather_fusion.2
  53.3 0.8 select_select_fusion
  54.2 5.6 %all-to-all-start.1 = ((bf16[16,4,1024]{2,1,0:T(4,128)(2,1)}), bf16[16,4,1024]{2,1,0:T(4,128)(2,1)S(1)}, u32[]{:S(2)}, u32[]{:S(2)}) async-start(bf16[16,4,1024]{2,1,0:T(4,128)(2,1)} %select_select_fusion), calls=%async_computation.2 | async-start | bytes 262144 | tf_op jit(solution)/shard_map/all_to_all | solution.py:89
  60.7 7.0 %all-to-all-done.1 = bf16[16,4,1024]{2,1,0:T(4,128)(2,1)S(1)} async-done(((bf16[16,4,1024]{2,1,0:T(4,128)(2,1)}), bf16[16,4,1024]{2,1,0:T(4,128)(2,1)S(1)}, u32[]{:S(2)}, u32[]{:S(2)}) %all-to-all-start.1) | async-done | bytes 131104 | tf_op jit(solution)/shard_map/all_to_all | solution.py:89
  68.2 8.2 %all_gather.16 = bf16[256,1024]{1,0:T(8,128)(2,1)S(1)} all-gather(bf16[128,1024]{1,0:T(8,128)(2,1)S(1)} %fusion.23), channel_id=1, replica_groups=mesh['exp'=16,'ctx'=2] {'ctx'}, dimensions={0}, use_global_device_ids=true | all-gather | bytes 786432 | tf_op jit(solution)/shard_map/all_gather | solution.py:116
  76.4 6.1 %all-gather.4.cloned.1.call-done = bf16[1024,512]{1,0:T(8,128)(2,1)} async-done(((bf16[64,512]{1,0:T(8,128)(2,1)}), bf16[1024,512]{1,0:T(8,128)(2,1)}) %all-gather.4.cloned.1.call-update) | async-done | bytes 1048592 | tf_op jit(solution)/shard_map/all_gather | solution.py:110
  82.4 38.9 %all-gather.6.cloned.1.call-done = bf16[1024,512]{1,0:T(8,128)(2,1)} async-done(((bf16[64,512]{1,0:T(8,128)(2,1)}), bf16[1024,512]{1,0:T(8,128)(2,1)}) %all-gather.6.cloned.1.call-update) | async-done | bytes 1048592 | tf_op jit(solution)/shard_map/all_gather | solution.py:111
  121.4 39.0 %all-gather.8.cloned.1.call-done = bf16[1024,512]{1,0:T(8,128)(2,1)} async-done(((bf16[64,512]{1,0:T(8,128)(2,1)}), bf16[1024,512]{1,0:T(8,128)(2,1)}) %all-gather.8.cloned.1.call-update) | async-done | bytes 1048592 | tf_op jit(solution)/shard_map/all_gather | solution.py:112
  160.3 2.8 %fusion.7 = bf16[256,1536]{1,0:T(8,128)(2,1)S(1)} fusion(bf16[256,1024]{1,0:T(8,128)(2,1)S(1)} %all_gather.16, bf16[1024,512]{1,0:T(8,128)(2,1)} %all-gather.8.cloned.1.call-done, bf16[1024,512]{1,0:T(8,128)(2,1)} %all-gather.6.cloned.1.call-done, bf16[1024,512]{1,0:T(8,128)(2,1)} %all-gather.4.cloned.1.call-done), kind=kOutput, calls=%fused_computation.10 | convolution fusion | flops 815136768 | bytes 4456448 | tf_op jit(solution)/shard_map/dot_general | solution.py:115
  164.0 0.9 fusion.57
  165.1 0.8 fusion.12
  166.0 8.2 %all_to_all.29 = bf16[2,128,512]{1,2,0:T(8,128)(2,1)S(1)} all-to-all(bf16[2,128,512]{1,2,0:T(8,128)(2,1)S(1)} %copy.99), channel_id=1, replica_groups=mesh['exp'=16,'ctx'=2] {'ctx'}, dimensions={0} | all-to-all | bytes 524288 | tf_op jit(solution)/shard_map/all_to_all | solution.py:149
  174.2 0.8 copy.100
  (81 shorter events, 7.0 us)
Async XLA Ops:
  8.0 35.3 %copy-start = (bf16[64,1024]{1,0:T(8,128)(2,1)S(1)}, bf16[64,1024]{1,0:T(8,128)(2,1)}, u32[]{:S(2)}) copy-start(bf16[64,1024]{1,0:T(8,128)(2,1)} %param.18) | copy-start | bytes 393220
  13.4 15.3 %all-to-all-start = ((bf16[16,4,1024]{2,1,0:T(4,128)(2,1)}), bf16[16,4,1024]{2,1,0:T(4,128)(2,1)S(1)}, u32[]{:S(2)}, u32[]{:S(2)}) async-start(bf16[16,4,1024]{2,1,0:T(4,128)(2,1)} %select_select_fusion.1), calls=%async_computation | async-start | bytes 262144 | tf_op jit(solution)/shard_map/all_to_all | solution.py:54
  20.9 30.7 %reduce-scatter.2.cloned.1.call-start = ((), (), s32[]{:S(2)}) async-start(), calls=%async_computation.4 | async-start | bytes 196608 | tf_op jit(solution)/shard_map/reduce_scatter | solution.py:68
  37.5 6.6 %copy-start.3 = (bf16[64,1024]{1,0:T(8,128)(2,1)S(1)}, bf16[64,1024]{1,0:T(8,128)(2,1)}, u32[]{:S(2)}) copy-start(bf16[64,1024]{1,0:T(8,128)(2,1)} %param.19) | copy-start | bytes 393220
  37.5 7.3 %copy-start.4 = (bf16[64,1024]{1,0:T(8,128)(2,1)S(1)}, bf16[64,1024]{1,0:T(8,128)(2,1)}, u32[]{:S(2)}) copy-start(bf16[64,1024]{1,0:T(8,128)(2,1)} %param.20) | copy-start | bytes 393220
  37.5 14.1 %copy-start.6 = (f32[2,16]{1,0:T(2,128)S(1)}, f32[2,16]{1,0:T(2,128)}, u32[]{:S(2)}) copy-start(f32[2,16]{1,0:T(2,128)} %param.13) | copy-start | bytes 388
  43.2 24.5 %copy-start.1 = (bf16[128,1024]{1,0:T(8,128)(2,1)S(1)}, bf16[128,1024]{1,0:T(8,128)(2,1)}, u32[]{:S(2)}) copy-start(bf16[128,1024]{1,0:T(8,128)(2,1)} %param.11) | copy-start | bytes 786436
  43.2 24.8 %copy-start.5 = (f32[1024]{0:T(1024)S(1)}, f32[1024]{0:T(1024)}, u32[]{:S(2)}) copy-start(f32[1024]{0:T(1024)} %param.17) | copy-start | bytes 12292
  43.3 39.2 %all-gather.4.cloned.1.call-start = ((), (), s32[]{:S(2)}) async-start(), calls=%async_computation.5 | async-start | bytes 1114112 | tf_op jit(solution)/shard_map/all_gather | solution.py:110
  44.0 77.4 %all-gather.6.cloned.1.call-start = ((), (), s32[]{:S(2)}) async-start(), calls=%async_computation.6 | async-start | bytes 1114112 | tf_op jit(solution)/shard_map/all_gather | solution.py:111
  44.7 115.6 %all-gather.8.cloned.1.call-start = ((), (), s32[]{:S(2)}) async-start(), calls=%async_computation.7 | async-start | bytes 1114112 | tf_op jit(solution)/shard_map/all_gather | solution.py:112
  54.2 13.5 %all-to-all-start.1 = ((bf16[16,4,1024]{2,1,0:T(4,128)(2,1)}), bf16[16,4,1024]{2,1,0:T(4,128)(2,1)S(1)}, u32[]{:S(2)}, u32[]{:S(2)}) async-start(bf16[16,4,1024]{2,1,0:T(4,128)(2,1)} %select_select_fusion), calls=%async_computation.2 | async-start | bytes 262144 | tf_op jit(solution)/shard_map/all_to_all | solution.py:89
  68.0 95.1 %copy-start.2 = (bf16[128,1024]{1,0:T(8,128)(2,1)}, bf16[128,1024]{1,0:T(8,128)(2,1)S(1)}, u32[]{:S(2)}) copy-start(bf16[128,1024]{1,0:T(8,128)(2,1)S(1)} %get-tuple-element.34) | copy-start | bytes 786436
Sparse Core Ops, SparseCore 0:
  43.4 8.1 reduce-scatter.1
Sparse Core Ops, SparseCore 1:
  45.9 36.5 all-gather.3
  84.5 36.8 all-gather.5
  123.4 36.9 all-gather.7
where the time goes:
time: 183 us
  waiting for transfers between devices  104 us (57%)
  blocking collectives  21.3 us (12%)
  between operations  16.6 us (9%)
  matrix products  14.1 us (8%)
  starting transfers between devices  13.2 us (7%)
  local copies, waits for them, and re-layouts  8.41 us (5%)
  other arithmetic  4.86 us (3%)
    all_gather x1, waiting for transfers between devices, local(): lax.all_gather(value_cols, 'exp', axis=0, tiled=True)  39 us
    all_gather x1, waiting for transfers between devices, local(): lax.all_gather(key_cols, 'exp', axis=0, tiled=True)  38.9 us
    all_to_all x1, blocking collectives, local(): lax.all_to_all(head_context.reshape(table_count, head_cols), 'ctx', split...  8.21 us
    all_gather x1, blocking collectives, local(): lax.all_gather(normed, 'ctx', axis=0, tiled=True)  8.17 us
    all_to_all x1, waiting for transfers between devices, local(): lax.all_to_all(outgoing, 'exp', split_axis=0, concat_axis=0, tiled=True)  7.65 us
    all_to_all x1, starting transfers between devices, local(): lax.all_to_all(outgoing, 'exp', split_axis=0, concat_axis=0, tiled=True)  7.41 us
    all_to_all x1, waiting for transfers between devices, local(): lax.all_to_all(reply_rows, 'exp', split_axis=0, concat_axis=0, tiled=True)  7.01 us
    all_gather x1, waiting for transfers between devices, local(): lax.all_gather(query_cols, 'exp', axis=0, tiled=True)  6.06 us
  transfers between devices with their start and end apart: 6, of which 6 were waited for; matrix products, arithmetic and copies ran while one was open for 3% of the time, Pallas kernels for 0%

commit v1 on v0

--- a/solution.py
+++ b/solution.py
@@ -1,6 +1,10 @@
+import functools
+
 import jax
 import jax.numpy as jnp
 from jax import lax
+from jax.experimental import pallas as pl
+from jax.experimental.pallas import tpu as pltpu
 from jax.sharding import PartitionSpec as P
 
 HEAD_DIM = 64
@@ -152,6 +156,560 @@
     return (layer_out, context)
 
 
+MESH = pl.DeviceIdType.MESH
+MOST = 2
+FOLD = 4
+NEVER = 1 << 20
+VMEM_LIMIT = 60 * 1024 * 1024
+
+
+def iota(shape, dim):
+    return lax.broadcasted_iota(jnp.int32, shape, dim)
+
+
+def onehot(condition):
+    return jnp.where(condition, 1.0, 0.0).astype(jnp.bfloat16)
+
+
+def dot(a, b):
+    return jnp.dot(a, b, preferred_element_type=jnp.float32)
+
+
+def dot_t(a, b, contract):
+    return lax.dot_general(a, b, (contract, ((), ())), preferred_element_type=jnp.float32)
+
+
+def fused(
+    exp_count,
+    ctx_count,
+    x_ref,
+    sel_ref,
+    gate_ref,
+    wg_hbm,
+    wu_hbm,
+    wd_hbm,
+    gain_ref,
+    q_hbm,
+    k_hbm,
+    v_hbm,
+    count_ref,
+    layer_ref,
+    context_ref,
+    wg,
+    wu,
+    wd,
+    weights,
+    out_rows,
+    in_rows,
+    reply_rows,
+    back_rows,
+    gates,
+    table,
+    proj,
+    away,
+    spread,
+    hbm_sem,
+    col_sem,
+    go_send,
+    go_recv,
+    back_send,
+    back_recv,
+    gate_send,
+    gate_recv,
+    z_send,
+    z_recv,
+    y_send,
+    y_recv,
+    c_send,
+    c_recv,
+    row_send,
+    row_recv,
+    out_send,
+    out_recv,
+):
+    e = lax.axis_index("exp")
+    c = lax.axis_index("ctx")
+    rows, width = x_ref.shape
+    experts, take = sel_ref.shape
+    local_experts = wg.shape[0]
+    devices = exp_count * ctx_count
+    me = e * ctx_count + c
+    group = local_experts * MOST
+    block = group * FOLD
+    fold = width // FOLD
+    shard = q_hbm.shape[0]
+    head_cols = width // ctx_count
+    padded = local_experts * devices * MOST
+
+    barrier = pltpu.get_barrier_semaphore()
+
+    def greet(d, carry):
+        to = lax.rem(me + d, devices)
+        pl.semaphore_signal(
+            barrier, inc=1, device_id=(to // ctx_count, lax.rem(to, ctx_count)), device_id_type=MESH
+        )
+        return carry
+
+    lax.fori_loop(1, devices, greet, 0)
+
+    def rows_of(o):
+        return weights.at[pl.ds(pl.multiple_of(o * shard, shard), shard), :]
+
+    own_cols = []
+    for n, ref in enumerate((q_hbm, k_hbm, v_hbm)):
+        copy = pltpu.make_async_copy(
+            ref.at[:, pl.ds(pl.multiple_of(c * head_cols, head_cols), head_cols)],
+            weights.at[
+                pl.ds(pl.multiple_of(e * shard, shard), shard), pl.ds(n * head_cols, head_cols)
+            ],
+            col_sem.at[n],
+        )
+        copy.start()
+        own_cols.append(copy)
+    loads = []
+    for x in range(local_experts):
+        for n, (hbm, vmem) in enumerate(((wg_hbm, wg), (wu_hbm, wu), (wd_hbm, wd))):
+            copy = pltpu.make_async_copy(hbm.at[x], vmem.at[x], hbm_sem.at[x * 3 + n])
+            copy.start()
+            loads.append(copy)
+
+    selected = sel_ref[...]
+    start = me * rows
+    mine = (selected >= start) & (selected < start + rows)
+    offset = selected - start
+    low = jnp.min(jnp.where(mine, offset, NEVER), axis=1, keepdims=True)
+    high = jnp.max(jnp.where(mine, offset, -1), axis=1, keepdims=True)
+    high = jnp.where(high == low, NEVER, high)
+    lanes = iota((experts, rows), 1)
+    picks = (onehot(lanes == low), onehot(lanes == high))
+
+    def spread_picks(count, per_expert_device):
+        m = iota((count, experts), 0)
+        j = m // (block * per_expert_device)
+        want = j * local_experts + lax.rem(m, group) // MOST
+        hit = iota((count, experts), 1) == want
+        rank = lax.rem(m, MOST)
+        return dot(onehot(hit & (rank == 0)), picks[0]) + dot(onehot(hit & (rank == 1)), picks[1])
+
+    out_count = exp_count * block
+    everything = dot(spread_picks(out_count, 1).astype(jnp.bfloat16), x_ref[...])
+    part = lax.rem(iota((out_count, 1), 0), block) // group
+    folded = jnp.zeros((out_count, fold), jnp.float32)
+    for f in range(FOLD):
+        folded = jnp.where(part == f, everything[:, f * fold : (f + 1) * fold], folded)
+    out_rows[...] = folded.astype(jnp.bfloat16)
+
+    in_count = devices * block
+    spread[...] = spread_picks(in_count, ctx_count).astype(jnp.bfloat16)
+
+    pair = iota((devices * MOST, 1), 0)
+    owner = pair // MOST
+    rank = lax.rem(pair, MOST)
+    for x in range(local_experts):
+        sel_x = sel_ref[pl.ds(e * local_experts + x, 1), :]
+        gate_x = gate_ref[pl.ds(x, 1), :]
+        off = jnp.broadcast_to(sel_x, (devices * MOST, take)) - owner * rows
+        own = (off >= 0) & (off < rows) & (lax.rem(owner, ctx_count) == c)
+        lo = jnp.min(jnp.where(own, off, NEVER), axis=1, keepdims=True)
+        hi = jnp.max(jnp.where(own, off, -1), axis=1, keepdims=True)
+        want = jnp.where(rank == 0, lo, jnp.where(hi == lo, NEVER, hi))
+        value = jnp.sum(
+            jnp.where(own & (off == want), jnp.broadcast_to(gate_x, off.shape), 0.0),
+            axis=1,
+            keepdims=True,
+        )
+        gates[0, x * devices * MOST : (x + 1) * devices * MOST, :] = jnp.broadcast_to(
+            value, (devices * MOST, gates.shape[2])
+        )
+
+    def slot(ref, index):
+        return ref.at[pl.ds(pl.multiple_of(index * block, block), block), :]
+
+    def go_copy(d):
+        to = lax.rem(me + d, devices)
+        return pltpu.make_async_remote_copy(
+            src_ref=slot(out_rows, to // ctx_count),
+            dst_ref=slot(in_rows, me),
+            send_sem=go_send.at[d],
+            recv_sem=go_recv.at[d],
+            device_id=(to // ctx_count, lax.rem(to, ctx_count)),
+            device_id_type=MESH,
+        )
+
+    def back_copy(d):
+        to = lax.rem(me + d, devices)
+        return pltpu.make_async_remote_copy(
+            src_ref=slot(reply_rows, to),
+            dst_ref=slot(back_rows, me),
+            send_sem=back_send.at[d],
+            recv_sem=back_recv.at[d],
+            device_id=(to // ctx_count, lax.rem(to, ctx_count)),
+            device_id_type=MESH,
+        )
+
+    def arrived(ref, sems, d):
+        source = lax.rem(me + devices - d, devices)
+        pltpu.make_async_remote_copy(
+            src_ref=slot(ref, source),
+            dst_ref=slot(ref, source),
+            send_sem=sems.at[d],
+            recv_sem=sems.at[d],
+            device_id=(source // ctx_count, lax.rem(source, ctx_count)),
+            device_id_type=MESH,
+        ).wait_recv()
+
+    def gate_copy(d):
+        return pltpu.make_async_remote_copy(
+            src_ref=gates.at[0],
+            dst_ref=gates.at[d],
+            send_sem=gate_send.at[d],
+            recv_sem=gate_recv.at[d],
+            device_id=(e, lax.rem(c + d, ctx_count)),
+            device_id_type=MESH,
+        )
+
+    depth = exp_count // 4
+    z, y, k = e // 4, lax.rem(e // 2, 2), lax.rem(e, 2)
+
+    def member(z_at, y_at, k_at):
+        return z_at * 4 + y_at * 2 + k_at
+
+    def weight_copy(o, to, send, recv):
+        return pltpu.make_async_remote_copy(
+            src_ref=rows_of(o),
+            dst_ref=rows_of(o),
+            send_sem=send,
+            recv_sem=recv,
+            device_id=(to, c),
+            device_id_type=MESH,
+        )
+
+    y_peer = member(z, 1 - y, k)
+    k_peer = member(z, y, 1 - k)
+
+    def z_copy(d):
+        return weight_copy(e, member(lax.rem(z + d, depth), y, k), z_send.at[d], z_recv.at[d])
+
+    def behind(d):
+        return lax.rem(z + depth - d, depth)
+
+    def y_copy(d):
+        return weight_copy(member(behind(d), y, k), y_peer, y_send.at[d], y_recv.at[d])
+
+    def y_in(d):
+        return weight_copy(member(behind(d), 1 - y, k), y_peer, y_send.at[d], y_recv.at[d])
+
+    def z_in(d):
+        return weight_copy(member(behind(d), y, k), y_peer, z_send.at[d], z_recv.at[d])
+
+    def k_copy(d, across):
+        y_at = 1 - y if across else y
+        n = d + depth * across
+        return weight_copy(member(behind(d), y_at, k), k_peer, c_send.at[n], c_recv.at[n])
+
+    def k_in(d, across):
+        y_at = 1 - y if across else y
+        n = d + depth * across
+        return weight_copy(member(behind(d), y_at, 1 - k), k_peer, c_send.at[n], c_recv.at[n])
+
+    def relay_z(d):
+        z_in(d).wait_recv()
+        y_copy(d).start()
+        k_copy(d, 0).start()
+
+    def relay_y(d):
+        y_in(d).wait_recv()
+        k_copy(d, 1).start()
+
+    pl.semaphore_wait(barrier, devices - 1)
+
+    def start_go(d, carry):
+        go_copy(d).start()
+        return carry
+
+    lax.fori_loop(1, devices, start_go, 0)
+    for d in range(1, ctx_count):
+        gate_copy(d).start()
+    for copy in own_cols:
+        copy.wait()
+    for d in range(1, depth):
+        z_copy(d).start()
+    y_copy(0).start()
+    k_copy(0, 0).start()
+
+    in_rows[pl.ds(pl.multiple_of(me * block, block), block), :] = out_rows[
+        pl.ds(pl.multiple_of(e * block, block), block), :
+    ]
+    m = iota((padded, in_count), 1)
+    n = iota((padded, in_count), 0)
+    per = devices * MOST
+    matches = (
+        (m // block == lax.rem(n, per) // MOST)
+        & (lax.rem(m, group) // MOST == n // per)
+        & (lax.rem(m, MOST) == lax.rem(n, MOST))
+    )
+    unfold = [
+        onehot(matches & (lax.rem(m, block) // group == f)) for f in range(FOLD)
+    ]
+
+    def wait_go(d, carry):
+        arrived(in_rows, go_recv, d)
+        return carry
+
+    lax.fori_loop(1, devices, wait_go, 0)
+    received = in_rows[...]
+    tokens = jnp.concatenate(
+        [dot(u, received).astype(jnp.bfloat16) for u in unfold], axis=1
+    )
+    for d in range(1, ctx_count):
+        gate_copy(d).wait_recv()
+    parts = []
+    for x in range(local_experts):
+        chosen = tokens[x * per : (x + 1) * per, :]
+        loads[3 * x].wait()
+        gate_part = dot(chosen, wg[x])
+        loads[3 * x + 1].wait()
+        up_part = dot(chosen, wu[x])
+        hidden = (gate_part / (1.0 + jnp.exp(-gate_part)) * up_part).astype(jnp.bfloat16)
+        loads[3 * x + 2].wait()
+        expert_out = dot(hidden, wd[x])
+        factor = gates[0, x * per : (x + 1) * per, 0:1]
+        for d in range(1, ctx_count):
+            factor = factor + gates[d, x * per : (x + 1) * per, 0:1]
+        parts.append((expert_out * factor).astype(jnp.bfloat16))
+        if x == 0:
+            for d in range(1, min(2, depth)):
+                relay_z(d)
+            relay_y(0)
+    weighted = jnp.concatenate(parts, axis=0)
+    m = iota((in_count, padded), 0)
+    n = iota((in_count, padded), 1)
+    back = onehot(
+        (m // block == lax.rem(n, per) // MOST)
+        & (lax.rem(m, group) // MOST == n // per)
+        & (lax.rem(m, MOST) == lax.rem(n, MOST))
+    )
+    part = lax.rem(iota((in_count, 1), 0), block) // group
+    folded = jnp.zeros((in_count, fold), jnp.float32)
+    for f in range(FOLD):
+        folded = jnp.where(part == f, dot(back, weighted[:, f * fold : (f + 1) * fold]), folded)
+    reply_rows[...] = folded.astype(jnp.bfloat16)
+
+    def start_back(d, carry):
+        back_copy(d).start()
+        return carry
+
+    lax.fori_loop(1, devices, start_back, 0)
+    back_rows[pl.ds(pl.multiple_of(me * block, block), block), :] = reply_rows[
+        pl.ds(pl.multiple_of(me * block, block), block), :
+    ]
+    for d in range(2, depth):
+        relay_z(d)
+
+    def wait_back(d, carry):
+        arrived(back_rows, back_recv, d)
+        return carry
+
+    lax.fori_loop(1, devices, wait_back, 0)
+    returned = back_rows[...]
+    moe = []
+    for f in range(FOLD):
+        hits = jnp.where(part == f, spread[...], jnp.zeros_like(spread[...]))
+        moe.append(dot_t(hits, returned, ((0,), (0,))))
+    layer = (x_ref[...].astype(jnp.float32) + jnp.concatenate(moe, axis=1)).astype(jnp.bfloat16)
+    layer_ref[...] = layer
+    widened = layer.astype(jnp.float32)
+    scale = lax.rsqrt(jnp.mean(widened * widened, axis=1, keepdims=True) + EPSILON)
+
+    def table_rows(index):
+        return pl.ds(pl.multiple_of(index * rows, rows), rows)
+
+    table[table_rows(c), :] = (widened * scale * gain_ref[...]).astype(jnp.bfloat16)
+
+    def row_copy(d, owner):
+        return pltpu.make_async_remote_copy(
+            src_ref=table.at[table_rows(owner), :],
+            dst_ref=table.at[table_rows(owner), :],
+            send_sem=row_send.at[d],
+            recv_sem=row_recv.at[d],
+            device_id=(e, lax.rem(c + d, ctx_count)),
+            device_id_type=MESH,
+        )
+
+    for d in range(1, ctx_count):
+        row_copy(d, c).start()
+    for d in range(1, depth):
+        relay_y(d)
+    for d in range(depth):
+        k_in(d, 0).wait_recv()
+        k_in(d, 1).wait_recv()
+
+    def project(owner):
+        normed = table[table_rows(owner), :]
+        for n in range(3):
+            cols = slice(n * head_cols, (n + 1) * head_cols)
+            proj[table_rows(owner), cols] = dot(normed, weights[:, cols]).astype(jnp.bfloat16)
+
+    project(c)
+    for d in range(1, ctx_count):
+        owner = lax.rem(c + ctx_count - d, ctx_count)
+        row_copy(d, owner).wait_recv()
+        project(owner)
+
+    total = table.shape[0]
+    allowed = iota((total, total), 1) < count_ref[0]
+    per_step = 128 // HEAD_DIM
+    steps = head_cols // 128
+
+    def out_copy(d, step):
+        to = lax.rem(c + d, ctx_count)
+        return pltpu.make_async_remote_copy(
+            src_ref=away.at[table_rows(to), step * 128 : (step + 1) * 128],
+            dst_ref=context_ref.at[
+                :, pl.ds(pl.multiple_of(c * head_cols + step * 128, 128), 128)
+            ],
+            send_sem=out_send.at[d, step],
+            recv_sem=out_recv.at[d, step],
+            device_id=(e, to),
+            device_id_type=MESH,
+        )
+
+    def out_in(d, step):
+        source = lax.rem(c + ctx_count - d, ctx_count)
+        cols = pl.ds(pl.multiple_of(source * head_cols + step * 128, 128), 128)
+        return pltpu.make_async_remote_copy(
+            src_ref=context_ref.at[:, cols],
+            dst_ref=context_ref.at[:, cols],
+            send_sem=out_send.at[d, step],
+            recv_sem=out_recv.at[d, step],
+            device_id=(e, source),
+            device_id_type=MESH,
+        )
+
+    for step in range(steps):
+        blended = []
+        for h in range(step * per_step, (step + 1) * per_step):
+            at = h * HEAD_DIM
+            query = proj[:, at : at + HEAD_DIM]
+            key = proj[:, head_cols + at : head_cols + at + HEAD_DIM]
+            value = proj[:, 2 * head_cols + at : 2 * head_cols + at + HEAD_DIM]
+            scores = dot_t(query, key, ((1,), (1,))) * (HEAD_DIM ** (-0.5))
+            scores = jnp.where(allowed, scores, MASKED)
+            top = jnp.max(scores, axis=1, keepdims=True)
+            raw = jnp.where(allowed, jnp.exp(scores - top), 0.0)
+            denominator = jnp.sum(raw, axis=1, keepdims=True)
+            blended.append(dot(raw.astype(jnp.bfloat16), value) / denominator)
+        away[:, step * 128 : (step + 1) * 128] = jnp.concatenate(blended, axis=1).astype(
+            jnp.bfloat16
+        )
+        for d in range(1, ctx_count):
+            out_copy(d, step).start()
+        context_ref[:, pl.ds(pl.multiple_of(c * head_cols + step * 128, 128), 128)] = away[
+            table_rows(c), step * 128 : (step + 1) * 128
+        ]
+
+    def wait_sends(d, carry):
+        go_copy(d).wait_send()
+        back_copy(d).wait_send()
+        return carry
+
+    lax.fori_loop(1, devices, wait_sends, 0)
+    for d in range(1, depth):
+        z_copy(d).wait_send()
+    for d in range(depth):
+        y_copy(d).wait_send()
+        k_copy(d, 0).wait_send()
+        k_copy(d, 1).wait_send()
+    for d in range(1, ctx_count):
+        gate_copy(d).wait_send()
+        row_copy(d, c).wait_send()
+        for step in range(steps):
+            out_copy(d, step).wait_send()
+            out_in(d, step).wait_recv()
+
+
+def fused_local(*operands):
+    inputs, selected, gate_weight, query_weight = (operands[i] for i in (0, 1, 3, 7))
+    exp_count = lax.axis_size("exp")
+    ctx_count = lax.axis_size("ctx")
+    rows, width = inputs.shape
+    local_experts, _, hidden = gate_weight.shape
+    devices = exp_count * ctx_count
+    block = local_experts * MOST * FOLD
+    head_cols = width // ctx_count
+    depth = exp_count // 4
+    padded = local_experts * devices * MOST
+    bf16 = jnp.bfloat16
+    dma = pltpu.SemaphoreType.DMA
+    vmem = pl.BlockSpec(memory_space=pltpu.VMEM)
+    hbm = pl.BlockSpec(memory_space=pl.ANY)
+    smem = pl.BlockSpec(memory_space=pltpu.SMEM)
+    operands = operands[:6] + (operands[6].reshape(1, width),) + operands[7:]
+    return pl.pallas_call(
+        functools.partial(fused, exp_count, ctx_count),
+        out_shape=(jax.ShapeDtypeStruct((rows, width), bf16),) * 2,
+        in_specs=[vmem, vmem, vmem, hbm, hbm, hbm, vmem, hbm, hbm, hbm, smem],
+        out_specs=(vmem, vmem),
+        scratch_shapes=[
+            pltpu.VMEM((local_experts, width, hidden), bf16),
+            pltpu.VMEM((local_experts, width, hidden), bf16),
+            pltpu.VMEM((local_experts, hidden, width), bf16),
+            pltpu.VMEM((width, 3 * head_cols), bf16),
+            pltpu.VMEM((exp_count * block, width // FOLD), bf16),
+            pltpu.VMEM((devices * block, width // FOLD), bf16),
+            pltpu.VMEM((devices * block, width // FOLD), bf16),
+            pltpu.VMEM((devices * block, width // FOLD), bf16),
+            pltpu.VMEM((ctx_count, padded, 128), jnp.float32),
+            pltpu.VMEM((ctx_count * rows, width), bf16),
+            pltpu.VMEM((ctx_count * rows, 3 * head_cols), bf16),
+            pltpu.VMEM((ctx_count * rows, head_cols), bf16),
+            pltpu.VMEM((devices * block, rows), bf16),
+            dma((3 * local_experts,)),
+            dma((3,)),
+            dma((devices,)),
+            dma((devices,)),
+            dma((devices,)),
+            dma((devices,)),
+            dma((ctx_count,)),
+            dma((ctx_count,)),
+            dma((depth,)),
+            dma((depth,)),
+            dma((depth,)),
+            dma((depth,)),
+            dma((2 * depth,)),
+            dma((2 * depth,)),
+            dma((ctx_count,)),
+            dma((ctx_count,)),
+            dma((ctx_count, head_cols // 128)),
+            dma((ctx_count, head_cols // 128)),
+        ],
+        compiler_params=pltpu.CompilerParams(
+            collective_id=0, has_side_effects=True, vmem_limit_bytes=VMEM_LIMIT
+        ),
+    )(*operands)
+
+
+def choose(*operands):
+    inputs, gate_weight = operands[0], operands[3]
+    exp_count, ctx_count = lax.axis_size("exp"), lax.axis_size("ctx")
+    rows, width = inputs.shape
+    local_experts = gate_weight.shape[0]
+    devices = exp_count * ctx_count
+    folded_rows = devices * local_experts * MOST * FOLD
+    table = rows * ctx_count
+    need = (
+        3 * 2 * gate_weight.size
+        + 6 * width * width // ctx_count
+        + 8 * folded_rows * width // FOLD
+        + 8 * FOLD * folded_rows * (folded_rows // FOLD)
+        + 12 * table * table
+    )
+    ranks = max(2, (2 * operands[1].shape[1] + exp_count - 1) // exp_count)
+    if exp_count % 4 == 0 and ranks == MOST and width // ctx_count % 128 == 0 and need < VMEM_LIMIT // 2:
+        return fused_local(*operands)
+    return local(*operands)
+
+
 def solution(mesh):
     placed = (
         P(("exp", "ctx"), None),
@@ -167,7 +725,7 @@
         P("exp"),
     )
     return jax.shard_map(
-        local,
+        choose,
         mesh=mesh,
         in_specs=placed,
         out_specs=(P(("exp", "ctx"), None), P(("exp", "ctx"), None)),

time: 183 us -> 58.1 us (0.32)
  waiting for transfers between devices: 104 us -> 0 us
  Pallas kernels: 0 us -> 51.8 us
  blocking collectives: 21.3 us -> 0 us
  between operations: 16.6 us -> 1.29 us
  matrix products: 14.1 us -> 0 us
  starting transfers between devices: 13.2 us -> 0 us
  other arithmetic: 4.86 us -> 0 us
  local copies, waits for them, and re-layouts: 8.41 us -> 4.72 us
    all_gather x3 -> x0, waiting for transfers between devices: 84 us -> none  [the longest x1 39 us: local(): lax.all_gather(value_cols, 'exp', axis=0, tiled=True)]
    pallas_call x0 -> x1, Pallas kernels: none -> 51.8 us  [fused_local(): pl.pallas_call(functools.partial(fused, exp_count, ctx_count), out_shape=...]
    all_to_all x2 -> x0, waiting for transfers between devices: 14.7 us -> none  [the longest x1 7.65 us: local(): lax.all_to_all(outgoing, 'exp', split_axis=0, concat_axis=0, tiled=True)]
    dot_general x6 -> x0, matrix products: 13.1 us -> none  [the longest x1 5.73 us: local(): jnp.einsum('nxf,xfd->nxd', hidden, down_weight, preferred_element_type=jn...]
    all_gather x2 -> x0, blocking collectives: 13.1 us -> none  [the longest x1 8.17 us: local(): lax.all_gather(normed, 'ctx', axis=0, tiled=True)]
    all_to_all x2 -> x0, starting transfers between devices: 13 us -> none  [the longest x1 7.41 us: local(): lax.all_to_all(outgoing, 'exp', split_axis=0, concat_axis=0, tiled=True)]
    all_to_all x1 -> x0, blocking collectives: 8.21 us -> none  [local(): lax.all_to_all(head_context.reshape(table_count, head_cols), 'ctx', split...]
    reduce_scatter x1 -> x0, waiting for transfers between devices: 5.52 us -> none  [local(): lax.psum_scatter(jnp.einsum('nxf,xfd->nxd', hidden, down_weight, preferre...]
  transfers between devices with their start and end apart: 6 -> 0, of which waited for: 6 -> 0; matrix products, arithmetic and copies ran while one was open for 3% -> 0% of each run, Pallas kernels for 0% -> 0%
where the time goes in v1:
time: 58.1 us; the launch traced here: 57.8 us
  Pallas kernels  51.8 us (89%)
  local copies, waits for them, and re-layouts  4.72 us (8%)
  between operations  1.29 us (2%)
    pallas_call x1, Pallas kernels, fused_local(): pl.pallas_call(functools.partial(fused, exp_count, ctx_count), out_shape=...  51.8 us
    unnamed x3, local copies, waits for them, and re-layouts  4.72 us

profile of v1, /device:TPU:0, one launch (start us, length us, event | category | flops | bytes accessed | tf_op | source)
XLA Modules:
  0.0 57.8 jit_solution(3542071549331396390)
XLA Ops:
  1.3 1.4 %copy.13.sel_ref = s32[32,16]{1,0:T(8,128)} copy(s32[32,16]{0,1:T(8,128)} %param.12) | data formatting | bytes 4096 | tf_op args[1]
  2.7 51.8 %shard_map.122 = (bf16[128,1024]{1,0:T(8,128)(2,1)}, bf16[128,1024]{1,0:T(8,128)(2,1)}) custom-call(bf16[128,1024]{1,0:T(8,128)(2,1)} %x_ref.1, s32[32,16]{1,0:T(8,128)} %copy.13.sel_ref, f32[2,16]{1,0:T(2,128)} %gate_ref.1, bf16[2,1024,1024]{2,1,0:T(8,128)(2,1)} %wg_hbm.1, bf16[2,1024,1024]{2,1,0:T(8,128)(2,1)} %wu_hbm.1, bf16[2,1024,1024]{2,1,0:T(8,128)(2,1)} %wd_hbm.1, ...), custom_call_target="tpu_custom_call" | custom-call | tf_op jit(solution)/shard_map/pallas_call | solution.py:648
  54.5 1.7 %copy.17 = bf16[128,1024]{1,0:T(8,128)(2,1)} copy(bf16[128,1024]{1,0:T(8,128)(2,1)} %get-tuple-element.4) | data formatting | bytes 524288
  56.1 1.7 %copy.18 = bf16[128,1024]{1,0:T(8,128)(2,1)} copy(bf16[128,1024]{1,0:T(8,128)(2,1)} %get-tuple-element.5) | data formatting | bytes 524288

commit v2 on v1

--- a/solution.py
+++ b/solution.py
@@ -230,7 +230,7 @@
     e = lax.axis_index("exp")
     c = lax.axis_index("ctx")
     rows, width = x_ref.shape
-    experts, take = sel_ref.shape
+    take, experts = sel_ref.shape
     local_experts = wg.shape[0]
     devices = exp_count * ctx_count
     me = e * ctx_count + c
@@ -277,22 +277,22 @@
     start = me * rows
     mine = (selected >= start) & (selected < start + rows)
     offset = selected - start
-    low = jnp.min(jnp.where(mine, offset, NEVER), axis=1, keepdims=True)
-    high = jnp.max(jnp.where(mine, offset, -1), axis=1, keepdims=True)
+    low = jnp.min(jnp.where(mine, offset, NEVER), axis=0, keepdims=True)
+    high = jnp.max(jnp.where(mine, offset, -1), axis=0, keepdims=True)
     high = jnp.where(high == low, NEVER, high)
-    lanes = iota((experts, rows), 1)
-    picks = (onehot(lanes == low), onehot(lanes == high))
-
-    def spread_picks(count, per_expert_device):
-        m = iota((count, experts), 0)
-        j = m // (block * per_expert_device)
-        want = j * local_experts + lax.rem(m, group) // MOST
-        hit = iota((count, experts), 1) == want
-        rank = lax.rem(m, MOST)
-        return dot(onehot(hit & (rank == 0)), picks[0]) + dot(onehot(hit & (rank == 1)), picks[1])
+    down = iota((rows, experts), 0)
+    picks = (onehot(down == low), onehot(down == high))
+
+    def taker(m, per_expert_device):
+        return m // (block * per_expert_device) * local_experts + lax.rem(m, group) // MOST
 
     out_count = exp_count * block
-    everything = dot(spread_picks(out_count, 1).astype(jnp.bfloat16), x_ref[...])
+    m = iota((out_count, experts), 0)
+    hit = iota((out_count, experts), 1) == taker(m, 1)
+    source = sum(
+        dot_t(onehot(hit & (lax.rem(m, MOST) == n)), picks[n], ((1,), (1,))) for n in range(MOST)
+    )
+    everything = dot(source.astype(jnp.bfloat16), x_ref[...])
     part = lax.rem(iota((out_count, 1), 0), block) // group
     folded = jnp.zeros((out_count, fold), jnp.float32)
     for f in range(FOLD):
@@ -300,13 +300,20 @@
     out_rows[...] = folded.astype(jnp.bfloat16)
 
     in_count = devices * block
-    spread[...] = spread_picks(in_count, ctx_count).astype(jnp.bfloat16)
+    m = iota((experts, in_count), 1)
+    hit = iota((experts, in_count), 0) == taker(m, ctx_count)
+    spread[...] = sum(
+        dot(picks[n], onehot(hit & (lax.rem(m, MOST) == n))) for n in range(MOST)
+    ).astype(jnp.bfloat16)
 
     pair = iota((devices * MOST, 1), 0)
     owner = pair // MOST
     rank = lax.rem(pair, MOST)
     for x in range(local_experts):
-        sel_x = sel_ref[pl.ds(e * local_experts + x, 1), :]
+        at_x = iota((take, experts), 1) == e * local_experts + x
+        column = jnp.sum(jnp.where(at_x, selected, 0), axis=1, keepdims=True)
+        same = iota((take, take), 0) == iota((take, take), 1)
+        sel_x = jnp.sum(jnp.where(same, column, 0), axis=0, keepdims=True)
         gate_x = gate_ref[pl.ds(x, 1), :]
         off = jnp.broadcast_to(sel_x, (devices * MOST, take)) - owner * rows
         own = (off >= 0) & (off < rows) & (lax.rem(owner, ctx_count) == c)
@@ -478,9 +485,9 @@
             factor = factor + gates[d, x * per : (x + 1) * per, 0:1]
         parts.append((expert_out * factor).astype(jnp.bfloat16))
         if x == 0:
+            relay_y(0)
             for d in range(1, min(2, depth)):
                 relay_z(d)
-            relay_y(0)
     weighted = jnp.concatenate(parts, axis=0)
     m = iota((in_count, padded), 0)
     n = iota((in_count, padded), 1)
@@ -512,10 +519,11 @@
 
     lax.fori_loop(1, devices, wait_back, 0)
     returned = back_rows[...]
+    along = lax.rem(iota((rows, in_count), 1), block) // group
     moe = []
     for f in range(FOLD):
-        hits = jnp.where(part == f, spread[...], jnp.zeros_like(spread[...]))
-        moe.append(dot_t(hits, returned, ((0,), (0,))))
+        hits = jnp.where(along == f, spread[...], jnp.zeros_like(spread[...]))
+        moe.append(dot(hits, returned))
     layer = (x_ref[...].astype(jnp.float32) + jnp.concatenate(moe, axis=1)).astype(jnp.bfloat16)
     layer_ref[...] = layer
     widened = layer.astype(jnp.float32)
@@ -626,6 +634,17 @@
         for step in range(steps):
             out_copy(d, step).wait_send()
             out_in(d, step).wait_recv()
+
+
+def emit(layer_ref, context_ref, layer_out, context_out, sem):
+    copies = [
+        pltpu.make_async_copy(layer_ref, layer_out, sem.at[0]),
+        pltpu.make_async_copy(context_ref, context_out, sem.at[1]),
+    ]
+    for copy in copies:
+        copy.start()
+    for copy in copies:
+        copy.wait()
 
 
 def fused_local(*operands):
@@ -644,8 +663,8 @@
     vmem = pl.BlockSpec(memory_space=pltpu.VMEM)
     hbm = pl.BlockSpec(memory_space=pl.ANY)
     smem = pl.BlockSpec(memory_space=pltpu.SMEM)
-    operands = operands[:6] + (operands[6].reshape(1, width),) + operands[7:]
-    return pl.pallas_call(
+    operands = operands[:1] + (operands[1].T,) + operands[2:6] + (operands[6].reshape(1, width),) + operands[7:]
+    results = pl.pallas_call(
         functools.partial(fused, exp_count, ctx_count),
         out_shape=(jax.ShapeDtypeStruct((rows, width), bf16),) * 2,
         in_specs=[vmem, vmem, vmem, hbm, hbm, hbm, vmem, hbm, hbm, hbm, smem],
@@ -663,7 +682,7 @@
             pltpu.VMEM((ctx_count * rows, width), bf16),
             pltpu.VMEM((ctx_count * rows, 3 * head_cols), bf16),
             pltpu.VMEM((ctx_count * rows, head_cols), bf16),
-            pltpu.VMEM((devices * block, rows), bf16),
+            pltpu.VMEM((rows, devices * block), bf16),
             dma((3 * local_experts,)),
             dma((3,)),
             dma((devices,)),
@@ -687,6 +706,13 @@
             collective_id=0, has_side_effects=True, vmem_limit_bytes=VMEM_LIMIT
         ),
     )(*operands)
+    return pl.pallas_call(
+        emit,
+        out_shape=(jax.ShapeDtypeStruct((rows, width), bf16),) * 2,
+        in_specs=[vmem, vmem],
+        out_specs=(hbm, hbm),
+        scratch_shapes=[dma((2,))],
+    )(*results)
 
 
 def choose(*operands):

time: 58.1 us -> 55.1 us (0.948)
  local copies, waits for them, and re-layouts: 4.72 us -> 0 us
  Pallas kernels: 51.8 us -> 53.6 us
    unnamed x3 -> x0, local copies, waits for them, and re-layouts: 4.72 us -> none
    pallas_call x0 -> x1, Pallas kernels: none -> 1.83 us  [fused_local(): pl.pallas_call(emit, out_shape=(jax.ShapeDtypeStruct((rows, width), bf16)...]
where the time goes in v2:
time: 55.1 us; the launch traced here: 54.9 us
  Pallas kernels  53.6 us (97%)
  between operations  1.29 us (2%)
    pallas_call x1, Pallas kernels, fused_local(): pl.pallas_call(functools.partial(fused, exp_count, ctx_count), out_shape=...  51.8 us
    pallas_call x1, Pallas kernels, fused_local(): pl.pallas_call(emit, out_shape=(jax.ShapeDtypeStruct((rows, width), bf16)...  1.83 us

profile of v2, /device:TPU:0, one launch (start us, length us, event | category | flops | bytes accessed | tf_op | source)
XLA Modules:
  0.0 54.9 jit_solution(13707607226364916398)
XLA Ops:
  1.3 51.8 %shard_map.122 = (bf16[128,1024]{1,0:T(8,128)(2,1)}, bf16[128,1024]{1,0:T(8,128)(2,1)}) custom-call(bf16[128,1024]{1,0:T(8,128)(2,1)} %x_ref.1, s32[16,32]{1,0:T(8,128)} %bitcast.2, f32[2,16]{1,0:T(2,128)} %gate_ref.1, bf16[2,1024,1024]{2,1,0:T(8,128)(2,1)} %wg_hbm.1, bf16[2,1024,1024]{2,1,0:T(8,128)(2,1)} %wu_hbm.1, bf16[2,1024,1024]{2,1,0:T(8,128)(2,1)} %wd_hbm.1, ...), custom_call_target="tpu_custom_call" | custom-call | tf_op jit(solution)/shard_map/pallas_call | solution.py:667
  53.1 1.8 %shard_map.123 = (bf16[128,1024]{1,0:T(8,128)(2,1)}, bf16[128,1024]{1,0:T(8,128)(2,1)}) custom-call(bf16[128,1024]{1,0:T(8,128)(2,1)} %get-tuple-element.4.layer_ref, bf16[128,1024]{1,0:T(8,128)(2,1)} %get-tuple-element.5.context_ref), custom_call_target="tpu_custom_call" | custom-call | tf_op jit(solution)/shard_map/pallas_call | solution.py:709

commit v3 on v2

--- a/solution.py
+++ b/solution.py
@@ -394,39 +394,75 @@
     y_peer = member(z, 1 - y, k)
     k_peer = member(z, y, 1 - k)
 
-    def z_copy(d):
-        return weight_copy(e, member(lax.rem(z + d, depth), y, k), z_send.at[d], z_recv.at[d])
-
-    def behind(d):
-        return lax.rem(z + depth - d, depth)
-
-    def y_copy(d):
-        return weight_copy(member(behind(d), y, k), y_peer, y_send.at[d], y_recv.at[d])
-
-    def y_in(d):
-        return weight_copy(member(behind(d), 1 - y, k), y_peer, y_send.at[d], y_recv.at[d])
-
-    def z_in(d):
-        return weight_copy(member(behind(d), y, k), y_peer, z_send.at[d], z_recv.at[d])
-
-    def k_copy(d, across):
+    def up_copy(t):
+        return weight_copy(member(z - t + 1, y, k), member(z + 1, y, k), z_send.at[0, t], z_recv.at[0, t])
+
+    def down_copy(t):
+        return weight_copy(member(z + t - 1, y, k), member(z - 1, y, k), z_send.at[1, t], z_recv.at[1, t])
+
+    def goes_up(t):
+        return (z + 1 < depth) & (z - t + 1 >= 0)
+
+    def goes_down(t):
+        return (z >= 1) & (z + t - 1 < depth)
+
+    def y_copy(at):
+        return weight_copy(member(at, y, k), y_peer, y_send.at[at], y_recv.at[at])
+
+    def y_in(at):
+        return weight_copy(member(at, 1 - y, k), y_peer, y_send.at[at], y_recv.at[at])
+
+    def k_copy(at, across):
         y_at = 1 - y if across else y
-        n = d + depth * across
-        return weight_copy(member(behind(d), y_at, k), k_peer, c_send.at[n], c_recv.at[n])
-
-    def k_in(d, across):
+        n = at + depth * across
+        return weight_copy(member(at, y_at, k), k_peer, c_send.at[n], c_recv.at[n])
+
+    def k_in(at, across):
         y_at = 1 - y if across else y
-        n = d + depth * across
-        return weight_copy(member(behind(d), y_at, 1 - k), k_peer, c_send.at[n], c_recv.at[n])
-
-    def relay_z(d):
-        z_in(d).wait_recv()
-        y_copy(d).start()
-        k_copy(d, 0).start()
-
-    def relay_y(d):
-        y_in(d).wait_recv()
-        k_copy(d, 1).start()
+        n = at + depth * across
+        return weight_copy(member(at, y_at, 1 - k), k_peer, c_send.at[n], c_recv.at[n])
+
+    def send_along(t):
+        @pl.when(goes_up(t))
+        def _():
+            up_copy(t).start()
+
+        @pl.when(goes_down(t))
+        def _():
+            down_copy(t).start()
+
+    def hop(t):
+        if t >= depth:
+            return
+
+        @pl.when(z - t >= 0)
+        def _():
+            weight_copy(member(z - t, y, k), k_peer, z_send.at[0, t], z_recv.at[0, t]).wait_recv()
+            if t + 1 < depth:
+
+                @pl.when(goes_up(t + 1))
+                def _():
+                    up_copy(t + 1).start()
+
+            y_copy(z - t).start()
+            k_copy(z - t, 0).start()
+
+        @pl.when(z + t < depth)
+        def _():
+            weight_copy(member(z + t, y, k), k_peer, z_send.at[1, t], z_recv.at[1, t]).wait_recv()
+            if t + 1 < depth:
+
+                @pl.when(goes_down(t + 1))
+                def _():
+                    down_copy(t + 1).start()
+
+            y_copy(z + t).start()
+            k_copy(z + t, 0).start()
+
+    def relay_y(i):
+        at = lax.rem(z + i, depth)
+        y_in(at).wait_recv()
+        k_copy(at, 1).start()
 
     pl.semaphore_wait(barrier, devices - 1)
 
@@ -439,10 +475,9 @@
         gate_copy(d).start()
     for copy in own_cols:
         copy.wait()
-    for d in range(1, depth):
-        z_copy(d).start()
-    y_copy(0).start()
-    k_copy(0, 0).start()
+    send_along(1)
+    y_copy(z).start()
+    k_copy(z, 0).start()
 
     in_rows[pl.ds(pl.multiple_of(me * block, block), block), :] = out_rows[
         pl.ds(pl.multiple_of(e * block, block), block), :
@@ -485,9 +520,8 @@
             factor = factor + gates[d, x * per : (x + 1) * per, 0:1]
         parts.append((expert_out * factor).astype(jnp.bfloat16))
         if x == 0:
+            hop(1)
             relay_y(0)
-            for d in range(1, min(2, depth)):
-                relay_z(d)
     weighted = jnp.concatenate(parts, axis=0)
     m = iota((in_count, padded), 0)
     n = iota((in_count, padded), 1)
@@ -510,8 +544,8 @@
     back_rows[pl.ds(pl.multiple_of(me * block, block), block), :] = reply_rows[
         pl.ds(pl.multiple_of(me * block, block), block), :
     ]
-    for d in range(2, depth):
-        relay_z(d)
+    for t in range(2, min(3, depth)):
+        hop(t)
 
     def wait_back(d, carry):
         arrived(back_rows, back_recv, d)
@@ -546,8 +580,10 @@
 
     for d in range(1, ctx_count):
         row_copy(d, c).start()
-    for d in range(1, depth):
-        relay_y(d)
+    for t in range(3, depth):
+        hop(t)
+    for i in range(1, depth):
+        relay_y(i)
     for d in range(depth):
         k_in(d, 0).wait_recv()
         k_in(d, 1).wait_recv()
@@ -622,8 +658,16 @@
         return carry
 
     lax.fori_loop(1, devices, wait_sends, 0)
-    for d in range(1, depth):
-        z_copy(d).wait_send()
+    for t in range(1, depth):
+
+        @pl.when(goes_up(t))
+        def _():
+            up_copy(t).wait_send()
+
+        @pl.when(goes_down(t))
+        def _():
+            down_copy(t).wait_send()
+
     for d in range(depth):
         y_copy(d).wait_send()
         k_copy(d, 0).wait_send()
@@ -691,8 +735,8 @@
             dma((devices,)),
             dma((ctx_count,)),
             dma((ctx_count,)),
-            dma((depth,)),
-            dma((depth,)),
+            dma((2, depth)),
+            dma((2, depth)),
             dma((depth,)),
             dma((depth,)),
             dma((2 * depth,)),

time: 55.1 us -> 50.3 us (0.913)
  Pallas kernels: 53.6 us -> 48.9 us
    pallas_call x1, Pallas kernels: 51.8 us -> 47.1 us  [fused_local(): pl.pallas_call(functools.partial(fused, exp_count, ctx_count), out_shape=...]
where the time goes in v3:
time: 50.3 us; the launch traced here: 50.2 us
  Pallas kernels  48.9 us (97%)
  between operations  1.29 us (3%)
    pallas_call x1, Pallas kernels, fused_local(): pl.pallas_call(functools.partial(fused, exp_count, ctx_count), out_shape=...  47.1 us
    pallas_call x1, Pallas kernels, fused_local(): pl.pallas_call(emit, out_shape=(jax.ShapeDtypeStruct((rows, width), bf16)...  1.83 us

profile of v3, /device:TPU:0, one launch (start us, length us, event | category | flops | bytes accessed | tf_op | source)
XLA Modules:
  0.0 50.2 jit_solution(449406727546847130)
XLA Ops:
  1.3 47.1 %shard_map.122 = (bf16[128,1024]{1,0:T(8,128)(2,1)}, bf16[128,1024]{1,0:T(8,128)(2,1)}) custom-call(bf16[128,1024]{1,0:T(8,128)(2,1)} %x_ref.1, s32[16,32]{1,0:T(8,128)} %bitcast.2, f32[2,16]{1,0:T(2,128)} %gate_ref.1, bf16[2,1024,1024]{2,1,0:T(8,128)(2,1)} %wg_hbm.1, bf16[2,1024,1024]{2,1,0:T(8,128)(2,1)} %wu_hbm.1, bf16[2,1024,1024]{2,1,0:T(8,128)(2,1)} %wd_hbm.1, ...), custom_call_target="tpu_custom_call" | custom-call | tf_op jit(solution)/shard_map/pallas_call | solution.py:711
  48.3 1.8 %shard_map.123 = (bf16[128,1024]{1,0:T(8,128)(2,1)}, bf16[128,1024]{1,0:T(8,128)(2,1)}) custom-call(bf16[128,1024]{1,0:T(8,128)(2,1)} %get-tuple-element.4.layer_ref, bf16[128,1024]{1,0:T(8,128)(2,1)} %get-tuple-element.5.context_ref), custom_call_target="tpu_custom_call" | custom-call | tf_op jit(solution)/shard_map/pallas_call | solution.py:753
